TPU v7x, 256 devices: a whole 4x4x8 slice. The times are simulated.
256 devices in a mesh: shard: 16 (over y, z_hi, core), rep: 16 (over x, z_lo).
Axes of the slice: x: 4, y: 4, z: 8 (z_hi: 2, z_lo: 4; z = z_hi * 4 + z_lo), core: 2. Of those that a mesh axis runs over, the one named last changes fastest.
Arguments:
- inputs: bfloat16 [50432, 768], P(('shard', 'rep')), may hold values from -6 to 6
- norm1_gain: float32 [768], replicated, may hold values from 0.25 to 1.75
- w_qkv: bfloat16 [768, 2304], P('shard'), may hold values from -0.21875 to 0.21875
- w_proj: bfloat16 [768, 768], P('shard'), may hold values from -0.875 to 0.875
- norm2_gain: float32 [768], replicated, may hold values from 0.25 to 1.75
- w_router: bfloat16 [768, 32], P('shard'), may hold values from -0.21875 to 0.21875
- w_expert_in: bfloat16 [2, 768, 3072], P(None, 'shard'), may hold values from -0.21875 to 0.21875
- w_expert_out: bfloat16 [2, 3072, 768], P(None, 'shard'), may hold values from -0.875 to 0.875
- expert_ids: int32 [50432, 2], P(('shard', 'rep')), may hold values from 0 to 1, all different within a row
- capacity: int32 [2], replicated, may hold values from 64 to 128, as said below
- cotangent: bfloat16 [50432, 768], P(('shard', 'rep')), may hold values from -6 to 6
Outputs:
- outputs: bfloat16 [50432, 768], P(('shard', 'rep'))
- grad_inputs: float32 [50432, 768], P(('shard', 'rep'))
- grad_norm1_gain: float32 [768], replicated
- grad_qkv: float32 [768, 2304], P('shard')
- grad_proj: float32 [768, 768], P('shard')
- grad_norm2_gain: float32 [768], replicated
- grad_router: float32 [768, 32], P('shard')
- grad_expert_in: float32 [2, 768, 3072], P(None, 'shard')
- grad_expert_out: float32 [2, 3072, 768], P(None, 'shard')
Inputs may be any that keep to these rules, and one draw needn't show every extreme that they name: Every expert's capacity is 64 to 128; some expert has exactly 128. `expert_ids`: the two experts of a token differ.
All inputs are finite; a program needn't handle non-finite values.
Results may differ from a plain program's by a relative error of at most 0.025.
Values may be sent and summed in bfloat16 or wider, within the bound.
No kernel may reach another device: no remote copies, remote signals or barrier semaphores. Data moves between devices by JAX's collectives and lax.ppermute only.
A program may use at most 128 MiB of HBM per device.

v0:
```python
import jax
import jax.numpy as jnp
from jax import lax
from jax.sharding import PartitionSpec as P

HEADS = 12
HD = 64
EXPERTS = 32
E_WIN = 2
SEQ = 197
CAP = 128
EPS = 1e-06


def layer_norm(values, gain):
    centred = values - jnp.mean(values, axis=-1, keepdims=True)
    inverse = lax.rsqrt(jnp.mean(centred * centred, axis=-1, keepdims=True) + EPS)
    normed = centred * inverse
    return (normed, inverse, (normed * gain).astype(jnp.bfloat16))


def layer_norm_back(grad_out, normed, inverse, gain):
    scaled = grad_out * gain
    grad_in = inverse * (
        scaled
        - jnp.mean(scaled, axis=-1, keepdims=True)
        - normed * jnp.mean(scaled * normed, axis=-1, keepdims=True)
    )
    return (grad_in, jnp.sum(grad_out * normed, axis=0))


def heads_view(block, images):
    return block.reshape(images, SEQ, HEADS, HD)


def attention_scores(qkv, images):
    width = HEADS * HD
    query = heads_view(qkv[:, :width], images)
    keys = heads_view(qkv[:, width : 2 * width], images)
    values = heads_view(qkv[:, 2 * width :], images)
    scores = jnp.einsum(
        "bqhd,bkhd->bhqk", query, keys, preferred_element_type=jnp.float32
    ) * HD ** (-0.5)
    return (query, keys, values, scores)


def attention_forward(qkv, images):
    query, keys, values, scores = attention_scores(qkv, images)
    logsum = jax.nn.logsumexp(scores, axis=-1, keepdims=True)
    probs = jnp.exp(scores - logsum).astype(jnp.bfloat16)
    mixed = jnp.einsum("bhqk,bkhd->bqhd", probs, values, preferred_element_type=jnp.float32).astype(
        jnp.bfloat16
    )
    return (mixed.reshape(images * SEQ, HEADS * HD), logsum)


def attention_backward(qkv, mixed, logsum, grad_mixed, images):
    query, keys, values, scores = attention_scores(qkv, images)
    probs_full = jnp.exp(scores - logsum)
    probs = probs_full.astype(jnp.bfloat16)
    grad_out = heads_view(grad_mixed, images)
    out_rows = heads_view(mixed, images)
    grad_values = jnp.einsum("bhqk,bqhd->bkhd", probs, grad_out, preferred_element_type=jnp.float32)
    grad_probs = jnp.einsum("bqhd,bkhd->bhqk", grad_out, values, preferred_element_type=jnp.float32)
    delta = jnp.sum(grad_out.astype(jnp.float32) * out_rows.astype(jnp.float32), axis=-1)
    delta = jnp.transpose(delta, (0, 2, 1))[..., None]
    grad_scores = (probs_full * (grad_probs - delta)).astype(jnp.bfloat16)
    scale = HD ** (-0.5)
    grad_query = (
        jnp.einsum("bhqk,bkhd->bqhd", grad_scores, keys, preferred_element_type=jnp.float32) * scale
    )
    grad_keys = (
        jnp.einsum("bhqk,bqhd->bkhd", grad_scores, query, preferred_element_type=jnp.float32)
        * scale
    )
    width = HEADS * HD
    rows = images * SEQ
    return jnp.concatenate(
        [
            grad_query.reshape(rows, width),
            grad_keys.reshape(rows, width),
            grad_values.reshape(rows, width),
        ],
        axis=1,
    ).astype(jnp.bfloat16)


def route_masks(expert_ids, capacity):
    count = expert_ids.shape[0]
    picked_hot = (expert_ids[:, :, None] == jnp.arange(E_WIN)[None, None, :]).astype(jnp.int32)
    ordered = jnp.transpose(picked_hot, (1, 0, 2)).reshape(2 * count, E_WIN)
    before = jnp.cumsum(ordered, axis=0) - ordered
    position = jnp.sum(before * ordered, axis=1).reshape(2, count).T
    limit = jnp.sum(picked_hot * capacity[None, None, :], axis=2)
    kept_mask = (position < limit).astype(jnp.float32)
    slot_hot = (position[:, :, None] == jnp.arange(CAP)[None, None, :]).astype(jnp.float32)
    return (
        kept_mask[:, :, None, None]
        * picked_hot.astype(jnp.float32)[:, :, :, None]
        * slot_hot[:, :, None, :]
    )


def body(
    inputs,
    norm1_gain,
    w_qkv,
    w_proj,
    norm2_gain,
    w_router,
    w_expert_in,
    w_expert_out,
    expert_ids,
    capacity,
    cotangent,
):
    high = lax.Precision.HIGHEST
    images = inputs.shape[0] // SEQ
    shard_rows = w_qkv.shape[0]
    hid_rows = w_expert_out.shape[1]
    full_qkv, full_proj, full_router = (
        lax.all_gather(w_qkv, "shard", axis=0, tiled=True),
        lax.all_gather(w_proj, "shard", axis=0, tiled=True),
        lax.all_gather(w_router, "shard", axis=0, tiled=True),
    )
    x_float = inputs.astype(jnp.float32)
    normed1, inverse1, hidden1 = layer_norm(x_float, norm1_gain)
    qkv = jnp.dot(hidden1, full_qkv, preferred_element_type=jnp.float32).astype(jnp.bfloat16)
    mixed, logsum = attention_forward(qkv, images)
    attended = x_float + jnp.dot(mixed, full_proj, preferred_element_type=jnp.float32)
    normed2, inverse2, hidden2 = layer_norm(attended, norm2_gain)
    logits = jnp.dot(hidden2, full_router, preferred_element_type=jnp.float32)
    router = jax.nn.softmax(logits, axis=-1)
    expert_hot = (expert_ids[:, :, None] == jnp.arange(EXPERTS)[None, None, :]).astype(jnp.float32)
    gate = jnp.sum(router[:, None, :] * expert_hot, axis=2)
    masks = route_masks(expert_ids, capacity)
    dispatch_float = jnp.sum(masks, axis=1)
    dispatch = dispatch_float.astype(jnp.bfloat16)
    combine = jnp.sum(masks * gate[:, :, None, None], axis=1)
    expert_rows = jnp.einsum(
        "rec,rd->ecd", dispatch, hidden2, preferred_element_type=jnp.float32
    ).astype(jnp.bfloat16)
    kept_weights = []
    pre_list = []
    activated_list = []
    eout_list = []
    for expert in range(E_WIN):
        first, second = (
            lax.all_gather(w_expert_in[expert], "shard", axis=0, tiled=True),
            lax.all_gather(w_expert_out[expert], "shard", axis=0, tiled=True),
        )
        kept_weights.append((first, second))
        pre = jnp.dot(expert_rows[expert], first, preferred_element_type=jnp.float32)
        activated = jax.nn.gelu(pre, approximate=False).astype(jnp.bfloat16)
        pre_list.append(pre)
        activated_list.append(activated)
        eout_list.append(
            jnp.dot(activated, second, preferred_element_type=jnp.float32).astype(jnp.bfloat16)
        )
    expert_out = jnp.stack(eout_list)
    eout_float = expert_out.astype(jnp.float32)
    moe = jnp.einsum("rec,ecd->rd", combine, eout_float, precision=high)
    outputs = (attended + moe).astype(jnp.bfloat16)
    grad = cotangent.astype(jnp.float32)
    matched = jnp.einsum("rd,ecd->rec", grad, eout_float, precision=high)
    grad_gate = jnp.sum(masks * matched[:, None, :, :], axis=(2, 3))
    grad_eout = jnp.einsum("rec,rd->ecd", combine, grad, precision=high).astype(jnp.bfloat16)
    back_qkv, back_proj, back_router = (full_qkv, full_proj, full_router)
    in_list = []
    out_list = []
    grad_rows_list = []
    for expert in range(E_WIN):
        first, second = kept_weights[expert]
        pre = pre_list[expert]
        grad_act = jnp.einsum(
            "cd,hd->ch", grad_eout[expert], second, preferred_element_type=jnp.float32
        )
        slope = (
            0.5 * (1.0 + jax.scipy.special.erf(pre * 0.7071067811865476))
            + pre * jnp.exp(-0.5 * pre * pre) * 0.3989422804014327
        )
        grad_pre = (grad_act * slope).astype(jnp.bfloat16)
        grad_rows_list.append(
            jnp.einsum("ch,dh->cd", grad_pre, first, preferred_element_type=jnp.float32).astype(
                jnp.bfloat16
            )
        )
        rows_here = expert_rows[expert]
        act_here = activated_list[expert]
        eout_here = grad_eout[expert]

        def in_term(start, count, rows_here=rows_here, grad_pre=grad_pre):
            return jnp.einsum("cd,ch->dh", rows_here, grad_pre, preferred_element_type=jnp.float32)

        def out_term(start, count, act_here=act_here, eout_here=eout_here):
            return jnp.einsum("ch,cd->hd", act_here, eout_here, preferred_element_type=jnp.float32)

        in_list.append(
            lax.psum_scatter(
                in_term(jnp.int32(0), shard_rows * lax.axis_size("shard")).astype(jnp.bfloat16),
                "shard",
                scatter_dimension=0,
                tiled=True,
            ).astype(jnp.float32)
        )
        out_list.append(
            lax.psum_scatter(
                out_term(jnp.int32(0), hid_rows * lax.axis_size("shard")).astype(jnp.bfloat16),
                "shard",
                scatter_dimension=0,
                tiled=True,
            ).astype(jnp.float32)
        )
    grad_rows = jnp.stack(grad_rows_list)
    grad_probs = jnp.sum(grad_gate[:, :, None] * expert_hot, axis=1)
    grad_logits = (
        router * (grad_probs - jnp.sum(router * grad_probs, axis=-1, keepdims=True))
    ).astype(jnp.bfloat16)
    grad_hidden2 = jnp.einsum(
        "rec,ecd->rd", dispatch, grad_rows, preferred_element_type=jnp.float32
    ) + jnp.einsum("re,de->rd", grad_logits, back_router, preferred_element_type=jnp.float32)
    grad_norm2, gain2 = layer_norm_back(grad_hidden2, normed2, inverse2, norm2_gain)
    grad_attended = grad + grad_norm2
    grad_branch = grad_attended.astype(jnp.bfloat16)
    grad_mixed = jnp.einsum(
        "rk,dk->rd", grad_branch, back_proj, preferred_element_type=jnp.float32
    ).astype(jnp.bfloat16)
    grad_qkv_rows = attention_backward(qkv, mixed, logsum, grad_mixed, images)
    grad_hidden1 = jnp.einsum(
        "rk,dk->rd", grad_qkv_rows, back_qkv, preferred_element_type=jnp.float32
    )
    grad_norm1, gain1 = layer_norm_back(grad_hidden1, normed1, inverse1, norm1_gain)
    grad_inputs = grad_attended + grad_norm1
    gain1_total, gain2_total = lax.psum((gain1, gain2), ("shard", "rep"))
    dense_local = lax.psum_scatter(
        jnp.concatenate(
            [
                jnp.einsum("rc,rk->ck", hidden1, grad_qkv_rows, preferred_element_type=jnp.float32),
                jnp.einsum("rc,rk->ck", mixed, grad_branch, preferred_element_type=jnp.float32),
                jnp.einsum("rc,rk->ck", hidden2, grad_logits, preferred_element_type=jnp.float32),
            ],
            axis=1,
        ).astype(jnp.bfloat16),
        "shard",
        scatter_dimension=0,
        tiled=True,
    )
    dense_total, in_total, out_total = (
        lax.psum(dense_local, "rep").astype(jnp.float32),
        lax.psum(jnp.stack(in_list).astype(jnp.bfloat16), "rep").astype(jnp.float32),
        lax.psum(jnp.stack(out_list).astype(jnp.bfloat16), "rep").astype(jnp.float32),
    )
    width = HEADS * HD
    return (
        outputs,
        grad_inputs,
        gain1_total,
        dense_total[:, : 3 * width],
        dense_total[:, 3 * width : 4 * width],
        gain2_total,
        dense_total[:, 4 * width :],
        in_total,
        out_total,
    )


def solution(mesh):
    in_specs = (
        P(("shard", "rep"), None),
        P(),
        P("shard", None),
        P("shard", None),
        P(),
        P("shard", None),
        P(None, "shard", None),
        P(None, "shard", None),
        P(("shard", "rep"), None),
        P(),
        P(("shard", "rep"), None),
    )
    out_specs = (
        P(("shard", "rep"), None),
        P(("shard", "rep"), None),
        P(),
        P("shard", None),
        P("shard", None),
        P(),
        P("shard", None),
        P(None, "shard", None),
        P(None, "shard", None),
    )
    return jax.shard_map(body, mesh=mesh, in_specs=in_specs, out_specs=out_specs, check_vma=False)
```

profile of v0, /device:TPU:24, one launch (start us, length us, event | category | flops | bytes accessed | tf_op | source)
XLA Modules:
  0.0 1204.1 jit_solution(413905897846838815)
XLA Ops:
  8.0 0.7 all-gather.14.cloned.1.call-update
  8.7 1.9 fusion.130
  10.7 0.9 fusion.129
  14.3 31.0 %all-gather.4 = bf16[16,48,32]{1,2,0:T(8,128)(2,1)S(1)} all-gather(bf16[1,48,32]{1,2,0:T(8,128)(2,1)S(1)} %bitcast.199), channel_id=1, replica_groups=mesh['shard'=16,'rep'=16] {'shard'}, dimensions={0}, use_global_device_ids=true | all-gather | bytes 52224 | tf_op jit(solution)/shard_map/all_gather | solution.py:124
  45.4 0.8 reshape.247
  47.8 39.1 %all-gather.12.cloned.1.call-done = bf16[768,2304]{1,0:T(8,128)(2,1)} async-done(((bf16[48,2304]{1,0:T(8,128)(2,1)}), bf16[768,2304]{1,0:T(8,128)(2,1)}) %all-gather.12.cloned.1.call-update) | async-done | bytes 3538960 | tf_op jit(solution)/shard_map/all_gather | solution.py:122
  86.8 3.0 convolution_convert_fusion.5
  89.9 0.9 copy.108
  90.8 0.9 copy.107
  91.9 1.8 multiply_reduce_fusion
  94.3 1.4 convolution_convert_fusion.10
  95.6 46.1 %all-gather.14.cloned.1.call-done = bf16[768,768]{1,0:T(8,128)(2,1)} async-done(((bf16[48,768]{1,0:T(8,128)(2,1)}), bf16[768,768]{1,0:T(8,128)(2,1)}) %all-gather.14.cloned.1.call-update) | async-done | bytes 1179664 | tf_op jit(solution)/shard_map/all_gather | solution.py:123
  141.7 1.9 fusion.131
  144.6 0.7 copy-done.6
  146.3 1.4 copy.113
  147.7 2.0 convolution_convert_fusion.9
  149.7 72.3 %all-gather.20.cloned.1.call-done = bf16[1,768,3072]{2,1,0:T(8,128)(2,1)} async-done(((bf16[1,48,3072]{2,1,0:T(8,128)(2,1)}), bf16[1,768,3072]{2,1,0:T(8,128)(2,1)}) %all-gather.20.cloned.1.call-update) | async-done | bytes 4718608 | tf_op jit(solution)/shard_map/all_gather | solution.py:149
  222.0 7.7 fusion.34
  229.7 71.5 %all-gather.22.cloned.1.call-done = bf16[1,3072,768]{2,1,0:T(8,128)(2,1)} async-done(((bf16[1,192,768]{2,1,0:T(8,128)(2,1)}), bf16[1,3072,768]{2,1,0:T(8,128)(2,1)}) %all-gather.22.cloned.1.call-update) | async-done | bytes 4718608 | tf_op jit(solution)/shard_map/all_gather | solution.py:150
  301.2 4.0 fusion.73
  305.2 75.7 %all-gather.16.cloned.1.call-done = bf16[1,768,3072]{2,1,0:T(8,128)(2,1)} async-done(((bf16[1,48,3072]{2,1,0:T(8,128)(2,1)}), bf16[1,768,3072]{2,1,0:T(8,128)(2,1)}) %all-gather.16.cloned.1.call-update) | async-done | bytes 4718608 | tf_op jit(solution)/shard_map/all_gather | solution.py:149
  380.9 7.9 fusion.31
  388.8 71.3 %all-gather.18.cloned.1.call-done = bf16[1,3072,768]{2,1,0:T(8,128)(2,1)} async-done(((bf16[1,192,768]{2,1,0:T(8,128)(2,1)}), bf16[1,3072,768]{2,1,0:T(8,128)(2,1)}) %all-gather.18.cloned.1.call-update) | async-done | bytes 4718608 | tf_op jit(solution)/shard_map/all_gather | solution.py:150
  460.1 3.4 fusion.79
  464.7 7.0 fusion.100
  472.9 0.7 copy-done.23
  473.7 3.7 convolution_convert_fusion
  477.4 4.7 convolution_convert_fusion.1
  482.3 4.8 fusion.22
  487.1 0.9 copy-done.12
  488.0 3.7 convolution_convert_fusion.2
  491.9 5.0 fusion.25
  496.9 0.9 copy-done.14
  497.8 3.5 convolution_convert_fusion.3
  501.4 1.6 copy.119
  503.7 4.3 fusion.82
  508.1 4.1 fusion.76
  513.4 0.8 copy-done
  514.2 1.3 convolution_convert_fusion.11
  515.5 1.9 copy.120
  517.4 2.0 copy.121
  519.4 1.1 convolution_convert_fusion.12
  520.6 0.8 copy.127
  521.4 1.4 multiply_reduce_fusion.1
  522.8 1.9 multiply_convert_fusion
  527.9 1.3 convolution_convert_fusion.4
  529.2 2.4 pad_maximum_fusion
  531.7 49.8 %reduce-scatter.14.cloned.1.call-done = bf16[192,768]{1,0:T(8,128)(2,1)} async-done(((bf16[3072,768]{1,0:T(8,128)(2,1)}), bf16[192,768]{1,0:T(8,128)(2,1)}) %reduce-scatter.14.cloned.1.call-update) | async-done | bytes 294928 | tf_op jit(solution)/shard_map/reduce_scatter | solution.py:207
  581.5 109.2 %reduce-scatter.12.cloned.1.call-done = bf16[192,768]{1,0:T(8,128)(2,1)} async-done(((bf16[3072,768]{1,0:T(8,128)(2,1)}), bf16[192,768]{1,0:T(8,128)(2,1)}) %reduce-scatter.12.cloned.1.call-update) | async-done | bytes 294928 | tf_op jit(solution)/shard_map/reduce_scatter | solution.py:207
  690.7 1.9 pad_maximum_fusion.3
  692.6 106.6 %reduce-scatter.10.cloned.1.call-done = bf16[48,3072]{1,0:T(8,128)(2,1)} async-done(((bf16[768,3072]{1,0:T(8,128)(2,1)}), bf16[48,3072]{1,0:T(8,128)(2,1)}) %reduce-scatter.10.cloned.1.call-update) | async-done | bytes 294928 | tf_op jit(solution)/shard_map/reduce_scatter | solution.py:199
  799.3 109.0 %reduce-scatter.8.cloned.1.call-done = bf16[48,3072]{1,0:T(8,128)(2,1)} async-done(((bf16[768,3072]{1,0:T(8,128)(2,1)}), bf16[48,3072]{1,0:T(8,128)(2,1)}) %reduce-scatter.8.cloned.1.call-update) | async-done | bytes 294928 | tf_op jit(solution)/shard_map/reduce_scatter | solution.py:199
  908.3 1.9 pad_maximum_fusion.2
  910.2 108.5 %reduce-scatter.6.cloned.1.call-done = bf16[48,3104]{1,0:T(8,128)(2,1)} async-done(((bf16[768,3104]{1,0:T(8,128)(2,1)}), bf16[48,3104]{1,0:T(8,128)(2,1)}) %reduce-scatter.6.cloned.1.call-update) | async-done | bytes 298000 | tf_op jit(solution)/shard_map/reduce_scatter | solution.py:235
  1018.8 4.2 fusion.96
  1022.9 74.5 %all-reduce.1 = (f32[768]{0:T(1024)}, f32[768]{0:T(1024)}) all-reduce(f32[768]{0:T(1024)S(1)} %get-tuple-element.56, f32[768]{0:T(1024)S(1)} %get-tuple-element.54), channel_id=1, replica_groups=mesh['shard'=16,'rep'=16] {'shard','rep'}, use_global_device_ids=true, to_apply=%region_24.25 | all-reduce | flops 1536 | bytes 12288 | tf_op jit(solution)/shard_map/psum | solution.py:234
  1098.8 1.1 fusion.60
  1100.0 1.1 fusion.95
  1101.1 88.9 %all-reduce.5.cloned.1.call-done = (bf16[48,3104]{1,0:T(8,128)(2,1)}, bf16[2,48,3072]{2,1,0:T(8,128)(2,1)}, bf16[2,192,768]{2,1,0:T(8,128)(2,1)}) async-done(((bf16[48,3104]{1,0:T(8,128)(2,1)}, bf16[2,48,3072]{2,1,0:T(8,128)(2,1)}, bf16[2,192,768]{2,1,0:T(8,128)(2,1)}), (bf16[48,3104]{1,0:T(8,128)(2,1)}, bf16[2,48,3072]{2,1,0:T(8,128)(2,1)}, bf16[2,192,768]{2,1,0:T(8,128)(2,1)})) %all-reduce.5.cloned.1.call-update) | async-done | bytes 1477648 | tf_op jit(solution)/shard_map/psum | solution.py:249
  1189.9 0.8 slice.86
  1190.7 1.6 slice.85
  1192.3 1.7 slice.84
  1194.7 1.1 convert_element_type.191
  1195.8 1.1 convert_element_type.194
  (179 shorter events, 17.6 us)
Async XLA Ops:
  7.2 3.5 copy-start.33
  7.2 79.7 %all-gather.12.cloned.1.call-start = ((), (), s32[]{:S(2)}) async-start(), calls=%async_computation.5 | async-start | bytes 3760128 | tf_op jit(solution)/shard_map/all_gather | solution.py:122
  7.9 133.8 %all-gather.14.cloned.1.call-start = ((), (), s32[]{:S(2)}) async-start(), calls=%async_computation.6 | async-start | bytes 1253376 | tf_op jit(solution)/shard_map/all_gather | solution.py:123
  8.7 4.2 copy-start.43
  8.7 213.3 %all-gather.20.cloned.1.call-start = ((), (), s32[]{:S(2)}) async-start(), calls=%async_computation.14 | async-start | bytes 5013504 | tf_op jit(solution)/shard_map/all_gather | solution.py:149
  10.6 3.7 copy-start.52
  10.6 35.6 %copy-start.53 = (s32[2]{0:T(128)S(1)}, s32[2]{0:T(128)}, u32[]{:S(2)}) copy-start(s32[2]{0:T(128)} %param.20) | copy-start | bytes 28
  10.7 35.8 %copy-start.3 = (bf16[197,768]{1,0:T(8,128)(2,1)S(1)}, bf16[197,768]{1,0:T(8,128)(2,1)}, u32[]{:S(2)}) copy-start(bf16[197,768]{1,0:T(8,128)(2,1)} %param.11) | copy-start | bytes 907780
  10.7 290.5 %all-gather.22.cloned.1.call-start = ((), (), s32[]{:S(2)}) async-start(), calls=%async_computation.15 | async-start | bytes 5013504 | tf_op jit(solution)/shard_map/all_gather | solution.py:150
  11.6 75.2 %copy-start.45 = (f32[768]{0:T(1024)S(1)}, f32[768]{0:T(1024)}, u32[]{:S(2)}) copy-start(f32[768]{0:T(1024)} %param.12) | copy-start | bytes 9220
  11.6 369.3 %all-gather.16.cloned.1.call-start = ((), (), s32[]{:S(2)}) async-start(), calls=%async_computation.12 | async-start | bytes 5013504 | tf_op jit(solution)/shard_map/all_gather | solution.py:149
  12.2 447.9 %all-gather.18.cloned.1.call-start = ((), (), s32[]{:S(2)}) async-start(), calls=%async_computation.13 | async-start | bytes 5013504 | tf_op jit(solution)/shard_map/all_gather | solution.py:150
  12.8 568.7 %reduce-scatter.14.cloned.1.call-start = ((), (), s32[]{:S(2)}) async-start(), calls=%async_computation.11 | async-start | bytes 5013504 | tf_op jit(solution)/shard_map/reduce_scatter | solution.py:207
  46.5 43.3 %copy-start.19 = (f32[197,2,2]{2,1,0:T(2,128)}, f32[197,2,2]{2,1,0:T(2,128)S(1)}, u32[]{:S(2)}) copy-start(f32[197,2,2]{2,1,0:T(2,128)S(1)} %copy.110) | copy-start | bytes 9460
  46.6 43.2 %copy-start.46 = (f32[197]{0:T(256)}, f32[197]{0:T(256)S(1)}, u32[]{:S(2)}) copy-start(f32[197]{0:T(256)S(1)} %broadcast_multiply_fusion.5) | copy-start | bytes 2368
  46.9 42.9 %copy-start.50 = (f32[197]{0:T(256)}, f32[197]{0:T(256)S(1)}, u32[]{:S(2)}) copy-start(f32[197]{0:T(256)S(1)} %add_rsqrt_fusion.1) | copy-start | bytes 2368
  47.2 42.7 %copy-start.21 = (f32[197,2,128]{2,1,0:T(2,128)}, f32[197,2,128]{2,1,0:T(2,128)S(1)}, u32[]{:S(2)}) copy-start(f32[197,2,128]{2,1,0:T(2,128)S(1)} %compare_convert_fusion) | copy-start | bytes 605188
  91.9 2.3 copy-start.8
  95.6 48.8 %copy-start.44 = (f32[768]{0:T(1024)S(1)}, f32[768]{0:T(1024)}, u32[]{:S(2)}) copy-start(f32[768]{0:T(1024)} %param.15) | copy-start | bytes 9220
  141.7 3.6 copy-start.34
  144.6 0.7 copy-start.6
  460.1 3.4 copy-start.24
  460.1 3.4 copy-start.26
  460.1 3.9 copy-start.36
  463.6 8.1 copy-start.28
  463.6 1.0 copy-start.20
  463.6 1.1 copy-start.22
  463.6 10.1 copy-start.5
  471.7 0.7 copy-start.17
  472.9 0.8 copy-start.23
  477.4 213.4 %reduce-scatter.12.cloned.1.call-start = ((), (), s32[]{:S(2)}) async-start(), calls=%async_computation.10 | async-start | bytes 5013504 | tf_op jit(solution)/shard_map/reduce_scatter | solution.py:207
  482.2 317.1 %reduce-scatter.10.cloned.1.call-start = ((), (), s32[]{:S(2)}) async-start(), calls=%async_computation.9 | async-start | bytes 5013504 | tf_op jit(solution)/shard_map/reduce_scatter | solution.py:199
  482.2 5.7 copy-start.15
  487.1 0.9 copy-start.12
  491.6 416.7 %reduce-scatter.8.cloned.1.call-start = ((), (), s32[]{:S(2)}) async-start(), calls=%async_computation.8 | async-start | bytes 5013504 | tf_op jit(solution)/shard_map/reduce_scatter | solution.py:199
  491.9 5.9 copy-start.16
  496.9 0.9 copy-start.14
  501.4 517.3 %reduce-scatter.6.cloned.1.call-start = ((), (), s32[]{:S(2)}) async-start(), calls=%async_computation.7 | async-start | bytes 5222400 | tf_op jit(solution)/shard_map/reduce_scatter | solution.py:235
  503.7 4.3 copy-start.13
  508.1 4.4 copy-start.35
  508.1 4.4 copy-start.49
  512.2 1.0 copy-start.25
  512.5 1.8 copy-start.7
  513.4 0.8 copy-start
  522.7 1.9 copy-start.11
  524.7 1.0 copy-start.10
  524.7 1.3 copy-start.1
  524.7 1.3 copy-start.4
  525.7 2.1 copy-start.39
  526.1 1.8 copy-start.41
  526.1 1.1 copy-start.9
  527.2 0.7 copy-start.51
  527.8 1.4 copy-start.37
  527.9 1.3 copy-start.30
  531.6 658.3 %all-reduce.5.cloned.1.call-start = ((), (), s32[]{:S(2)}) async-start(), calls=%async_computation.16 | async-start | bytes 2973696 | tf_op jit(solution)/shard_map/psum | solution.py:249
  692.6 326.1 %copy-start.38 = (bf16[12,64,197]{2,1,0:T(8,128)(2,1)S(1)}, bf16[12,64,197]{2,1,0:T(8,128)(2,1)}, u32[]{:S(2)}) copy-start(bf16[12,64,197]{2,1,0:T(8,128)(2,1)} %copy-done.37) | copy-start | bytes 907780
  692.6 326.1 %copy-start.40 = (bf16[12,64,197]{2,1,0:T(8,128)(2,1)S(1)}, bf16[12,64,197]{2,1,0:T(8,128)(2,1)}, u32[]{:S(2)}) copy-start(bf16[12,64,197]{2,1,0:T(8,128)(2,1)} %copy-done.39) | copy-start | bytes 907780
  692.6 326.1 %copy-start.42 = (bf16[12,64,197]{2,1,0:T(8,128)(2,1)S(1)}, bf16[12,64,197]{2,1,0:T(8,128)(2,1)}, u32[]{:S(2)}) copy-start(bf16[12,64,197]{2,1,0:T(8,128)(2,1)} %copy-done.41) | copy-start | bytes 907780
  1018.7 80.1 %copy-start.18 = (f32[197,2,128]{2,1,0:T(2,128)S(1)}, f32[197,2,128]{2,1,0:T(2,128)}, u32[]{:S(2)}) copy-start(f32[197,2,128]{2,1,0:T(2,128)} %copy-done.17) | copy-start | bytes 605188
  1018.7 80.1 %copy-start.27 = (bf16[1,128,768]{2,1,0:T(8,128)(2,1)S(1)}, bf16[1,128,768]{2,1,0:T(8,128)(2,1)}, u32[]{:S(2)}) copy-start(bf16[1,128,768]{2,1,0:T(8,128)(2,1)} %fusion.73) | copy-start | bytes 589828
  1018.8 80.1 %copy-start.29 = (bf16[1,128,768]{2,1,0:T(8,128)(2,1)S(1)}, bf16[1,128,768]{2,1,0:T(8,128)(2,1)}, u32[]{:S(2)}) copy-start(bf16[1,128,768]{2,1,0:T(8,128)(2,1)} %copy-done.28) | copy-start | bytes 589828
  1022.9 77.1 %copy-start.2 = (f32[197,768]{1,0:T(8,128)S(1)}, f32[197,768]{1,0:T(8,128)}, u32[]{:S(2)}) copy-start(f32[197,768]{1,0:T(8,128)} %copy-done) | copy-start | bytes 1815556
  1189.9 4.8 copy-start.32
  1189.9 5.9 copy-start.31
  (2 other events, 1.2 us)
Sparse Core Ops, SparseCore 0:
  10.7 76.0 all-gather.11
  89.5 52.1 all-gather.13
  145.0 76.9 all-gather.19
  224.6 76.5 all-gather.21
  304.3 76.5 all-gather.15
  383.5 76.5 all-gather.17
  477.5 103.9 reduce-scatter.13
  586.5 104.1 reduce-scatter.11
  695.1 104.1 reduce-scatter.9
  804.1 104.1 reduce-scatter.7
  912.8 105.8 reduce-scatter.5
  1022.5 167.3 all-reduce.4
where the time goes:
time: 1210 us; the launch traced here: 1200 us
  waiting for transfers between devices  951 us (79%)
  blocking collectives  106 us (9%)
  matrix products  81.6 us (7%)
  local copies, waits for them, and re-layouts  26.4 us (2%)
  other arithmetic  24 us (2%)
  between operations  15.4 us (1%)
    reduce_scatter x2, waiting for transfers between devices, body(): lax.psum_scatter(in_term(jnp.int32(0), shard_rows * lax.axis_size('shard'...  216 us
    reduce_scatter x2, waiting for transfers between devices, body(): lax.psum_scatter(out_term(jnp.int32(0), hid_rows * lax.axis_size('shard')...  159 us
    all_gather x2, waiting for transfers between devices, body(): lax.all_gather(w_expert_in[expert], 'shard', axis=0, tiled=True)  148 us
    all_gather x2, waiting for transfers between devices, body(): lax.all_gather(w_expert_out[expert], 'shard', axis=0, tiled=True)  143 us
    reduce_scatter x1, waiting for transfers between devices, body(): lax.psum_scatter(jnp.concatenate([jnp.einsum('rc,rk->ck', hidden1, grad_q...  108 us
    psum x1, waiting for transfers between devices, body(): lax.psum(dense_local, 'rep').astype(jnp.float32)  88.9 us
    psum x1, blocking collectives, body(): gain1_total, gain2_total = lax.psum((gain1, gain2), ('shard', 'rep'))  74.5 us
    all_gather x1, waiting for transfers between devices, body(): lax.all_gather(w_proj, 'shard', axis=0, tiled=True)  46.1 us
  transfers between devices with their start and end apart: 12, of which 12 were waited for; matrix products, arithmetic and copies ran while one was open for 9% of the time, Pallas kernels for 0%

commit v1 on v0

--- a/solution.py
+++ b/solution.py
@@ -246,7 +246,7 @@
         tiled=True,
     )
     dense_total, in_total, out_total = (
-        lax.psum(dense_local, "rep").astype(jnp.float32),
+        jnp.sum(lax.all_gather(dense_local, "rep"), axis=0).astype(jnp.float32),
         lax.psum(jnp.stack(in_list).astype(jnp.bfloat16), "rep").astype(jnp.float32),
         lax.psum(jnp.stack(out_list).astype(jnp.bfloat16), "rep").astype(jnp.float32),
     )

time: 1210 us -> 1320 us (1.091)
  waiting for transfers between devices: 951 us -> 1060 us
    all_gather x0 -> x1, waiting for transfers between devices: none -> 113 us  [body(): lax.all_gather(dense_local, 'rep')]
  transfers between devices with their start and end apart: 12 -> 13, of which waited for: 12 -> 13; matrix products, arithmetic and copies ran while one was open for 9% -> 8% of each run, Pallas kernels for 0% -> 0%
where the time goes in v1:
time: 1320 us; the launch traced here: 1310 us
  waiting for transfers between devices  1060 us (80%)
  blocking collectives  105 us (8%)
  matrix products  81.8 us (6%)
  other arithmetic  28.3 us (2%)
  local copies, waits for them, and re-layouts  23.7 us (2%)
  between operations  15 us (1%)
    reduce_scatter x2, waiting for transfers between devices, body(): lax.psum_scatter(in_term(jnp.int32(0), shard_rows * lax.axis_size('shard'...  216 us
    reduce_scatter x2, waiting for transfers between devices, body(): lax.psum_scatter(out_term(jnp.int32(0), hid_rows * lax.axis_size('shard')...  159 us
    all_gather x2, waiting for transfers between devices, body(): lax.all_gather(w_expert_in[expert], 'shard', axis=0, tiled=True)  148 us
    all_gather x2, waiting for transfers between devices, body(): lax.all_gather(w_expert_out[expert], 'shard', axis=0, tiled=True)  143 us
    all_gather x1, waiting for transfers between devices, body(): lax.all_gather(dense_local, 'rep')  113 us
    reduce_scatter x1, waiting for transfers between devices, body(): lax.psum_scatter(jnp.concatenate([jnp.einsum('rc,rk->ck', hidden1, grad_q...  108 us
    psum x1, waiting for transfers between devices, body(): lax.psum(jnp.stack(in_list).astype(jnp.bfloat16), 'rep').astype(jnp.float32)  84.8 us
    psum x1, blocking collectives, body(): gain1_total, gain2_total = lax.psum((gain1, gain2), ('shard', 'rep'))  74.4 us
  transfers between devices with their start and end apart: 13, of which 13 were waited for; matrix products, arithmetic and copies ran while one was open for 8% of the time, Pallas kernels for 0%

profile of v1, /device:TPU:24, one launch (start us, length us, event | category | flops | bytes accessed | tf_op | source)
XLA Modules:
  0.0 1313.7 jit_solution(9555919561906572955)
XLA Ops:
  8.7 1.9 fusion.130
  10.7 0.9 fusion.129
  14.3 31.0 %all-gather.5 = bf16[16,48,32]{1,2,0:T(8,128)(2,1)S(1)} all-gather(bf16[1,48,32]{1,2,0:T(8,128)(2,1)S(1)} %bitcast.201), channel_id=1, replica_groups=mesh['shard'=16,'rep'=16] {'shard'}, dimensions={0}, use_global_device_ids=true | all-gather | bytes 52224 | tf_op jit(solution)/shard_map/all_gather | solution.py:124
  45.4 0.8 reshape.248
  47.8 39.1 %all-gather.14.cloned.1.call-done = bf16[768,2304]{1,0:T(8,128)(2,1)} async-done(((bf16[48,2304]{1,0:T(8,128)(2,1)}), bf16[768,2304]{1,0:T(8,128)(2,1)}) %all-gather.14.cloned.1.call-update) | async-done | bytes 3538960 | tf_op jit(solution)/shard_map/all_gather | solution.py:122
  86.8 3.0 convolution_convert_fusion.5
  89.9 0.9 copy.110
  90.8 0.9 copy.109
  91.9 1.8 multiply_reduce_fusion
  94.3 1.4 convolution_convert_fusion.10
  95.6 46.1 %all-gather.16.cloned.1.call-done = bf16[768,768]{1,0:T(8,128)(2,1)} async-done(((bf16[48,768]{1,0:T(8,128)(2,1)}), bf16[768,768]{1,0:T(8,128)(2,1)}) %all-gather.16.cloned.1.call-update) | async-done | bytes 1179664 | tf_op jit(solution)/shard_map/all_gather | solution.py:123
  141.7 1.9 fusion.131
  144.6 0.7 copy-done.6
  146.3 1.4 copy.115
  147.7 2.0 convolution_convert_fusion.9
  149.7 72.3 %all-gather.22.cloned.1.call-done = bf16[1,768,3072]{2,1,0:T(8,128)(2,1)} async-done(((bf16[1,48,3072]{2,1,0:T(8,128)(2,1)}), bf16[1,768,3072]{2,1,0:T(8,128)(2,1)}) %all-gather.22.cloned.1.call-update) | async-done | bytes 4718608 | tf_op jit(solution)/shard_map/all_gather | solution.py:149
  222.0 7.7 fusion.34
  229.7 71.5 %all-gather.24.cloned.1.call-done = bf16[1,3072,768]{2,1,0:T(8,128)(2,1)} async-done(((bf16[1,192,768]{2,1,0:T(8,128)(2,1)}), bf16[1,3072,768]{2,1,0:T(8,128)(2,1)}) %all-gather.24.cloned.1.call-update) | async-done | bytes 4718608 | tf_op jit(solution)/shard_map/all_gather | solution.py:150
  301.2 4.0 fusion.73
  305.2 75.7 %all-gather.18.cloned.1.call-done = bf16[1,768,3072]{2,1,0:T(8,128)(2,1)} async-done(((bf16[1,48,3072]{2,1,0:T(8,128)(2,1)}), bf16[1,768,3072]{2,1,0:T(8,128)(2,1)}) %all-gather.18.cloned.1.call-update) | async-done | bytes 4718608 | tf_op jit(solution)/shard_map/all_gather | solution.py:149
  380.9 8.1 fusion.31
  389.1 71.0 %all-gather.20.cloned.1.call-done = bf16[1,3072,768]{2,1,0:T(8,128)(2,1)} async-done(((bf16[1,192,768]{2,1,0:T(8,128)(2,1)}), bf16[1,3072,768]{2,1,0:T(8,128)(2,1)}) %all-gather.20.cloned.1.call-update) | async-done | bytes 4718608 | tf_op jit(solution)/shard_map/all_gather | solution.py:150
  460.1 3.4 fusion.79
  464.7 7.0 fusion.100
  472.9 0.7 copy-done.23
  473.7 3.7 convolution_convert_fusion
  477.4 4.8 convolution_convert_fusion.1
  482.3 4.8 fusion.22
  487.1 0.9 copy-done.12
  488.0 3.6 convolution_convert_fusion.2
  491.9 5.0 fusion.25
  496.9 0.9 copy-done.14
  497.7 3.5 convolution_convert_fusion.3
  501.3 1.6 copy.121
  502.9 0.7 select_reduce_fusion
  503.6 4.3 fusion.82
  508.0 4.1 fusion.76
  513.3 0.8 copy-done
  514.1 1.3 convolution_convert_fusion.11
  515.4 1.9 copy.122
  517.3 2.0 copy.123
  519.3 1.1 convolution_convert_fusion.12
  520.5 0.8 copy.129
  521.3 1.4 multiply_reduce_fusion.1
  522.7 1.9 multiply_convert_fusion
  527.8 1.3 convolution_convert_fusion.4
  529.1 2.4 pad_maximum_fusion
  531.6 49.9 %reduce-scatter.14.cloned.1.call-done = bf16[192,768]{1,0:T(8,128)(2,1)} async-done(((bf16[3072,768]{1,0:T(8,128)(2,1)}), bf16[192,768]{1,0:T(8,128)(2,1)}) %reduce-scatter.14.cloned.1.call-update) | async-done | bytes 294928 | tf_op jit(solution)/shard_map/reduce_scatter | solution.py:207
  581.5 109.2 %reduce-scatter.12.cloned.1.call-done = bf16[192,768]{1,0:T(8,128)(2,1)} async-done(((bf16[3072,768]{1,0:T(8,128)(2,1)}), bf16[192,768]{1,0:T(8,128)(2,1)}) %reduce-scatter.12.cloned.1.call-update) | async-done | bytes 294928 | tf_op jit(solution)/shard_map/reduce_scatter | solution.py:207
  690.7 1.9 pad_maximum_fusion.3
  692.6 106.6 %reduce-scatter.10.cloned.1.call-done = bf16[48,3072]{1,0:T(8,128)(2,1)} async-done(((bf16[768,3072]{1,0:T(8,128)(2,1)}), bf16[48,3072]{1,0:T(8,128)(2,1)}) %reduce-scatter.10.cloned.1.call-update) | async-done | bytes 294928 | tf_op jit(solution)/shard_map/reduce_scatter | solution.py:199
  799.2 109.0 %reduce-scatter.8.cloned.1.call-done = bf16[48,3072]{1,0:T(8,128)(2,1)} async-done(((bf16[768,3072]{1,0:T(8,128)(2,1)}), bf16[48,3072]{1,0:T(8,128)(2,1)}) %reduce-scatter.8.cloned.1.call-update) | async-done | bytes 294928 | tf_op jit(solution)/shard_map/reduce_scatter | solution.py:199
  908.2 1.9 pad_maximum_fusion.2
  910.2 108.3 %reduce-scatter.6.cloned.1.call-done = bf16[48,3104]{1,0:T(8,128)(2,1)} async-done(((bf16[768,3104]{1,0:T(8,128)(2,1)}), bf16[48,3104]{1,0:T(8,128)(2,1)}) %reduce-scatter.6.cloned.1.call-update) | async-done | bytes 298000 | tf_op jit(solution)/shard_map/reduce_scatter | solution.py:235
  1018.6 4.2 fusion.96
  1022.8 74.4 %all-reduce.1 = (f32[768]{0:T(1024)}, f32[768]{0:T(1024)}) all-reduce(f32[768]{0:T(1024)S(1)} %get-tuple-element.56, f32[768]{0:T(1024)S(1)} %get-tuple-element.54), channel_id=1, replica_groups=mesh['shard'=16,'rep'=16] {'shard','rep'}, use_global_device_ids=true, to_apply=%region_24.25 | all-reduce | flops 1536 | bytes 12288 | tf_op jit(solution)/shard_map/psum | solution.py:234
  1098.5 1.1 fusion.60
  1099.6 1.1 fusion.95
  1100.7 84.8 %all-reduce.5.cloned.1.call-done = (bf16[2,48,3072]{2,1,0:T(8,128)(2,1)}, bf16[2,192,768]{2,1,0:T(8,128)(2,1)}) async-done(((bf16[2,48,3072]{2,1,0:T(8,128)(2,1)}, bf16[2,192,768]{2,1,0:T(8,128)(2,1)}), (bf16[2,48,3072]{2,1,0:T(8,128)(2,1)}, bf16[2,192,768]{2,1,0:T(8,128)(2,1)})) %all-reduce.5.cloned.1.call-update) | async-done | bytes 1179664 | tf_op jit(solution)/shard_map/psum | solution.py:250
  1185.5 2.2 convert_element_type.193
  1187.7 1.1 convert_element_type.196
  1188.8 112.8 %all-gather.26.cloned.1.call-done = bf16[768,3104]{1,0:T(8,128)(2,1)} async-done(((bf16[48,3104]{1,0:T(8,128)(2,1)}), bf16[768,3104]{1,0:T(8,128)(2,1)}) %all-gather.26.cloned.1.call-update) | async-done | bytes 4767760 | tf_op jit(solution)/shard_map/all_gather | solution.py:249
  1301.6 3.2 reduce_sum.224
  1305.5 0.8 slice.84
  (181 shorter events, 18.3 us)
Async XLA Ops:
  7.2 3.5 copy-start.32
  7.2 79.7 %all-gather.14.cloned.1.call-start = ((), (), s32[]{:S(2)}) async-start(), calls=%async_computation.5 | async-start | bytes 3760128 | tf_op jit(solution)/shard_map/all_gather | solution.py:122
  7.9 133.8 %all-gather.16.cloned.1.call-start = ((), (), s32[]{:S(2)}) async-start(), calls=%async_computation.6 | async-start | bytes 1253376 | tf_op jit(solution)/shard_map/all_gather | solution.py:123
  8.7 4.2 copy-start.42
  8.7 213.3 %all-gather.22.cloned.1.call-start = ((), (), s32[]{:S(2)}) async-start(), calls=%async_computation.14 | async-start | bytes 5013504 | tf_op jit(solution)/shard_map/all_gather | solution.py:149
  10.6 3.7 copy-start.51
  10.6 35.6 %copy-start.52 = (s32[2]{0:T(128)S(1)}, s32[2]{0:T(128)}, u32[]{:S(2)}) copy-start(s32[2]{0:T(128)} %param.20) | copy-start | bytes 28
  10.7 35.8 %copy-start.3 = (bf16[197,768]{1,0:T(8,128)(2,1)S(1)}, bf16[197,768]{1,0:T(8,128)(2,1)}, u32[]{:S(2)}) copy-start(bf16[197,768]{1,0:T(8,128)(2,1)} %param.11) | copy-start | bytes 907780
  10.7 290.5 %all-gather.24.cloned.1.call-start = ((), (), s32[]{:S(2)}) async-start(), calls=%async_computation.15 | async-start | bytes 5013504 | tf_op jit(solution)/shard_map/all_gather | solution.py:150
  11.6 75.2 %copy-start.44 = (f32[768]{0:T(1024)S(1)}, f32[768]{0:T(1024)}, u32[]{:S(2)}) copy-start(f32[768]{0:T(1024)} %param.12) | copy-start | bytes 9220
  11.6 369.3 %all-gather.18.cloned.1.call-start = ((), (), s32[]{:S(2)}) async-start(), calls=%async_computation.12 | async-start | bytes 5013504 | tf_op jit(solution)/shard_map/all_gather | solution.py:149
  12.2 447.9 %all-gather.20.cloned.1.call-start = ((), (), s32[]{:S(2)}) async-start(), calls=%async_computation.13 | async-start | bytes 5013504 | tf_op jit(solution)/shard_map/all_gather | solution.py:150
  12.8 568.8 %reduce-scatter.14.cloned.1.call-start = ((), (), s32[]{:S(2)}) async-start(), calls=%async_computation.11 | async-start | bytes 5013504 | tf_op jit(solution)/shard_map/reduce_scatter | solution.py:207
  46.5 43.3 %copy-start.19 = (f32[197,2,2]{2,1,0:T(2,128)}, f32[197,2,2]{2,1,0:T(2,128)S(1)}, u32[]{:S(2)}) copy-start(f32[197,2,2]{2,1,0:T(2,128)S(1)} %copy.112) | copy-start | bytes 9460
  46.6 43.2 %copy-start.45 = (f32[197]{0:T(256)}, f32[197]{0:T(256)S(1)}, u32[]{:S(2)}) copy-start(f32[197]{0:T(256)S(1)} %broadcast_multiply_fusion.5) | copy-start | bytes 2368
  46.9 42.9 %copy-start.49 = (f32[197]{0:T(256)}, f32[197]{0:T(256)S(1)}, u32[]{:S(2)}) copy-start(f32[197]{0:T(256)S(1)} %add_rsqrt_fusion.1) | copy-start | bytes 2368
  47.2 42.7 %copy-start.21 = (f32[197,2,128]{2,1,0:T(2,128)}, f32[197,2,128]{2,1,0:T(2,128)S(1)}, u32[]{:S(2)}) copy-start(f32[197,2,128]{2,1,0:T(2,128)S(1)} %compare_convert_fusion) | copy-start | bytes 605188
  91.9 2.3 copy-start.8
  95.6 48.8 %copy-start.43 = (f32[768]{0:T(1024)S(1)}, f32[768]{0:T(1024)}, u32[]{:S(2)}) copy-start(f32[768]{0:T(1024)} %param.15) | copy-start | bytes 9220
  141.7 3.6 copy-start.33
  144.6 0.7 copy-start.6
  460.1 3.4 copy-start.24
  460.1 3.4 copy-start.26
  460.1 3.9 copy-start.35
  463.6 8.1 copy-start.28
  463.6 1.0 copy-start.20
  463.6 1.1 copy-start.22
  463.6 10.1 copy-start.5
  471.7 0.7 copy-start.17
  472.9 0.8 copy-start.23
  477.4 213.3 %reduce-scatter.12.cloned.1.call-start = ((), (), s32[]{:S(2)}) async-start(), calls=%async_computation.10 | async-start | bytes 5013504 | tf_op jit(solution)/shard_map/reduce_scatter | solution.py:207
  482.2 317.0 %reduce-scatter.10.cloned.1.call-start = ((), (), s32[]{:S(2)}) async-start(), calls=%async_computation.9 | async-start | bytes 5013504 | tf_op jit(solution)/shard_map/reduce_scatter | solution.py:199
  482.3 5.7 copy-start.15
  487.1 0.9 copy-start.12
  491.6 416.6 %reduce-scatter.8.cloned.1.call-start = ((), (), s32[]{:S(2)}) async-start(), calls=%async_computation.8 | async-start | bytes 5013504 | tf_op jit(solution)/shard_map/reduce_scatter | solution.py:199
  491.9 5.9 copy-start.16
  496.8 0.9 copy-start.14
  501.3 517.2 %reduce-scatter.6.cloned.1.call-start = ((), (), s32[]{:S(2)}) async-start(), calls=%async_computation.7 | async-start | bytes 5222400 | tf_op jit(solution)/shard_map/reduce_scatter | solution.py:235
  503.6 4.3 copy-start.13
  508.0 4.4 copy-start.34
  508.0 4.4 copy-start.48
  512.1 1.0 copy-start.25
  512.4 1.8 copy-start.7
  513.3 0.8 copy-start
  522.6 1.9 copy-start.11
  524.6 1.0 copy-start.10
  524.6 1.3 copy-start.1
  524.6 1.3 copy-start.4
  525.6 2.1 copy-start.38
  526.0 1.8 copy-start.40
  526.0 1.1 copy-start.9
  527.1 0.7 copy-start.50
  527.7 1.4 copy-start.36
  527.8 1.3 copy-start.30
  531.5 654.0 %all-reduce.5.cloned.1.call-start = ((), (), s32[]{:S(2)}) async-start(), calls=%async_computation.17 | async-start | bytes 2359296 | tf_op jit(solution)/shard_map/psum | solution.py:250
  692.6 325.9 %copy-start.37 = (bf16[12,64,197]{2,1,0:T(8,128)(2,1)S(1)}, bf16[12,64,197]{2,1,0:T(8,128)(2,1)}, u32[]{:S(2)}) copy-start(bf16[12,64,197]{2,1,0:T(8,128)(2,1)} %copy-done.36) | copy-start | bytes 907780
  692.6 325.9 %copy-start.39 = (bf16[12,64,197]{2,1,0:T(8,128)(2,1)S(1)}, bf16[12,64,197]{2,1,0:T(8,128)(2,1)}, u32[]{:S(2)}) copy-start(bf16[12,64,197]{2,1,0:T(8,128)(2,1)} %copy-done.38) | copy-start | bytes 907780
  692.6 325.9 %copy-start.41 = (bf16[12,64,197]{2,1,0:T(8,128)(2,1)S(1)}, bf16[12,64,197]{2,1,0:T(8,128)(2,1)}, u32[]{:S(2)}) copy-start(bf16[12,64,197]{2,1,0:T(8,128)(2,1)} %copy-done.40) | copy-start | bytes 907780
  910.1 391.4 %all-gather.26.cloned.1.call-start = ((), (), s32[]{:S(2)}) async-start(), calls=%async_computation.16 | async-start | bytes 5222400 | tf_op jit(solution)/shard_map/all_gather | solution.py:249
  1018.6 79.9 %copy-start.18 = (f32[197,2,128]{2,1,0:T(2,128)S(1)}, f32[197,2,128]{2,1,0:T(2,128)}, u32[]{:S(2)}) copy-start(f32[197,2,128]{2,1,0:T(2,128)} %copy-done.17) | copy-start | bytes 605188
  1018.6 79.9 %copy-start.27 = (bf16[1,128,768]{2,1,0:T(8,128)(2,1)S(1)}, bf16[1,128,768]{2,1,0:T(8,128)(2,1)}, u32[]{:S(2)}) copy-start(bf16[1,128,768]{2,1,0:T(8,128)(2,1)} %fusion.73) | copy-start | bytes 589828
  1018.6 79.9 %copy-start.29 = (bf16[1,128,768]{2,1,0:T(8,128)(2,1)S(1)}, bf16[1,128,768]{2,1,0:T(8,128)(2,1)}, u32[]{:S(2)}) copy-start(bf16[1,128,768]{2,1,0:T(8,128)(2,1)} %copy-done.28) | copy-start | bytes 589828
  1022.8 76.9 %copy-start.2 = (f32[197,768]{1,0:T(8,128)S(1)}, f32[197,768]{1,0:T(8,128)}, u32[]{:S(2)}) copy-start(f32[197,768]{1,0:T(8,128)} %copy-done) | copy-start | bytes 1815556
  1185.5 2.2 copy-start.31
  (2 other events, 1.2 us)
Sparse Core Ops, SparseCore 0:
  10.7 76.0 all-gather.13
  89.5 52.1 all-gather.15
  145.0 76.9 all-gather.21
  224.6 76.5 all-gather.23
  304.3 76.5 all-gather.17
  383.5 76.5 all-gather.19
  477.5 103.9 reduce-scatter.13
  586.5 104.1 reduce-scatter.11
  695.1 104.0 reduce-scatter.9
  804.0 104.1 reduce-scatter.7
  912.7 105.7 reduce-scatter.5
  1022.2 163.2 all-reduce.4
  1187.3 114.2 all-gather.25
